TPU v7x, 32 devices: a whole 2x2x4 slice. The times are simulated.
32 devices in a mesh: grp: 2 (over y), field: 4 (over z), pair: 4 (over x, core).
Axes of the slice: x: 2, y: 2, z: 4, core: 2. Of those that a mesh axis runs over, the one named last changes fastest.
Arguments:
- cholesky_tensor: float32 [1536, 9216], P(('grp', 'field'), 'pair'), parts along dimension 0, may hold values from -0.0625 to 0.0625
- green_function: float32 [2, 8192, 9216], P(None, ('grp', 'field'), 'pair'), parts along dimension 1, may hold values from -6 to 6
- mean_field: float32 [2, 1536], P(None, 'grp'), parts along dimension 1, may hold values from -6 to 6
- field_noise: float32 [8192, 768], P(('grp', 'field')), parts along dimension 0, may hold values from -6 to 6
Outputs:
- capped_bias: float32 [2, 8192, 768], P(None, ('grp', 'field', 'pair')), parts along dimension 1
- one_body: float32 [8192, 2, 9216], P(('grp', 'field'), None, 'pair'), parts along dimension 0
There are 2 independent parts, one for each index of `grp`. A program takes and returns all parts, laid end to end along the dimension named above; each array names one. Nothing has to cross between parts.
All inputs are finite; a program needn't handle non-finite values.
Results may differ from a plain program's by a relative error of at most 0.000059.
Values sent between devices are 32-bit elements; how exact they have to be, the bound alone decides.
A program may use at most 128 MiB of HBM per device.

v0:
```python
import functools
import math

import jax
import jax.numpy as jnp
from jax import lax
from jax.experimental import pallas as pl
from jax.experimental.pallas import tpu as pltpu
from jax.sharding import PartitionSpec as P

LANES = 128


def split(x):
    high = x.astype(jnp.bfloat16)
    return high, (x - high.astype(jnp.float32)).astype(jnp.bfloat16)


MESH = pl.DeviceIdType.MESH


def bias_kernel(
    n_field, n_pair, late, chol_in, green, noise, mean_ref, share_ref, chol_out, capped_out, early_out,
    stack, green_split, staging, right, part, first, second, capped, mean_turned, noise_tile, left_high, left_low,
    ring_send, ring_recv, part_send, part_recv, sum_send, sum_recv, own_send, own_recv,
    peer_send, peer_recv, pass_send, pass_recv, load_sem, green_sem, chol_sem, capped_sem, noise_sem, early_sem,
):
    fields, pairs = stack.shape
    share = share_ref.shape[1]
    block = chol_in.shape[0]
    chunk = math.gcd(block, LANES)
    chunks, own = fields // chunk, block // chunk
    granules, per_granule = fields // LANES, LANES // chunk
    half = n_pair // 2
    me_field, me_pair = lax.axis_index("field"), lax.axis_index("pair")
    left_id = {"field": lax.rem(me_field + n_field - 1, n_field)}
    right_id = {"field": lax.rem(me_field + 1, n_field)}
    core, hop = lax.rem(me_pair, 2), me_pair // 2
    partner_id = {"pair": me_pair + 1 - 2 * core}

    def peer_hop(d):
        return lax.rem(hop + d, half)

    def peer_id(d):
        return {"pair": 2 * peer_hop(d) + core}

    barrier = pltpu.get_barrier_semaphore()
    others = [left_id, right_id, partner_id] + [peer_id(d) for d in range(1, half)]
    for other in others:
        pl.semaphore_signal(barrier, inc=1, device_id=other, device_id_type=MESH)
    pl.semaphore_wait(barrier, len(others))

    def remote(source, target, send, recv, device):
        return pltpu.make_async_remote_copy(
            src_ref=source, dst_ref=target, send_sem=send, recv_sem=recv, device_id=device, device_id_type=MESH
        )

    def ring(k):
        source = chol_in.at[pl.ds(k * chunk, chunk)] if k < own else stack.at[pl.ds(k * chunk, chunk)]
        target = stack.at[pl.ds((k + own) * chunk, chunk)]
        return remote(source, target, ring_send.at[k], ring_recv.at[k + own], left_id)

    for k in range(min(own, chunks - own)):
        ring(k).start()
    load = pltpu.make_async_copy(chol_in, stack.at[pl.ds(0, block)], load_sem)
    load.start()
    early = granules - late
    turn = lax.rem(fields - me_field * block, fields)

    def noise_copy(j):
        return pltpu.make_async_copy(noise.at[pl.ds(j * share, share)], noise_tile, noise_sem)

    noise_copy(0).start()
    mean_turned[...] = pltpu.roll(mean_ref[...], turn, 1)

    def fetch(t):
        j, c = t // 2, t % 2
        return pltpu.make_async_copy(green.at[c, pl.ds(j * share, share)], staging.at[t % 2], green_sem.at[t % 2])

    fetch(0).start()
    for t in range(2 * n_pair):
        if t + 1 < 2 * n_pair:
            fetch(t + 1).start()
        fetch(t).wait()

        @pl.loop(0, share // 16)
        def _(step):
            at = pl.multiple_of(step * 16, 16)
            high, low = split(staging[t % 2, pl.ds(at, 16), :])
            into = pl.multiple_of(t * share + at, 16)
            green_split[pl.ds(into, 16), :pairs] = high
            green_split[pl.ds(into, 16), pairs:] = low

    load.wait()

    def part_copy(g):
        return remote(part.at[g, 1 - core], first.at[g], part_send.at[g], part_recv.at[g], partner_id)

    def sum_copy(g, d):
        source = part.at[g, core, peer_hop(d)]
        return remote(source, second.at[g, d - 1], sum_send.at[g, d - 1], sum_recv.at[g, d - 1], peer_id(d))

    def own_copy(g):
        at = capped.at[g, core, hop]
        return remote(at, at, own_send.at[g], own_recv.at[g], partner_id)

    def peer_copy(g, d):
        at = capped.at[g, core, hop]
        return remote(at, at, peer_send.at[g, d - 1], peer_recv.at[g, d - 1], peer_id(d))

    def pass_copy(g, d):
        at = capped.at[g, core, peer_hop(half - d)]
        return remote(at, at, pass_send.at[g, d - 1], pass_recv.at[g, d - 1], partner_id)

    def chol_copy(g):
        return pltpu.make_async_copy(right.at[g], chol_out.at[g - early], chol_sem.at[g - early])

    def capped_copy(g):
        return pltpu.make_async_copy(capped.at[g], capped_out.at[g - early], capped_sem.at[g - early])

    def products(g):
        for k in range(g * per_granule, (g + 1) * per_granule):
            if k >= own:
                ring(k - own).wait_recv()
                if k + own < chunks:
                    ring(k).start()
        step_rows = 32
        for at in range(0, LANES, step_rows):
            high, low = split(stack[g * LANES + at : g * LANES + at + step_rows, :])
            right[g, 0, at : at + step_rows, :] = high
            right[g, 1, at : at + step_rows, :] = low
        if g >= early:
            chol_copy(g).start()

        @pl.loop(0, n_pair)
        def _(j):
            rows = pl.ds(pl.multiple_of(j * 2 * share, 16), 2 * share)
            dims = (((1,), (1,)), ((), ()))
            pair_of = right[g].reshape(2 * LANES, pairs)
            both = lax.dot_general(green_split[rows, :pairs], pair_of, dims, preferred_element_type=jnp.float32)
            cross = lax.dot_general(green_split[rows, pairs:], right[g, 0], dims, preferred_element_type=jnp.float32)
            total = both[:, :LANES] + both[:, LANES:] + cross
            part[g, lax.rem(j, 2), j // 2] = total.reshape(2, share, LANES)

        part_copy(g).start()

    def add_partner(g):
        part_copy(g).wait()
        for d in list(range(1, half)) + [0]:
            at = peer_hop(d)
            part[g, core, at] = part[g, core, at] + first[g, at]
            if d:
                sum_copy(g, d).start()

    def cap(g):
        total = part[g, core, hop]
        for d in range(1, half):
            sum_copy(g, d).wait()
            total = total + second[g, d - 1]
        columns = slice(g * LANES, (g + 1) * LANES)
        value = 2.0 * jnp.tanh((total - mean_turned[:, columns][:, None, :]) / 2.0)
        capped[g, core, hop] = value
        share_ref[:, :, columns] = value
        for d in range(1, half):
            peer_copy(g, d).start()
        own_copy(g).start()

    def hand_on(g):
        for d in range(1, half):
            peer_copy(g, d).wait()
            pass_copy(g, d).start()

    def finish(g):
        own_copy(g).wait()
        for d in range(1, half):
            pass_copy(g, d).wait()
        if g >= early:
            capped_copy(g).start()

    def early_copy(t):
        return pltpu.make_async_copy(staging.at[t % 2], early_out.at[t // 2, t % 2], early_sem.at[t % 2])

    def early_products():
        cut = 256 if pairs % 256 == 0 else LANES
        for j in range(n_pair):
            noise_copy(j).wait()
            for c in range(2):
                t = 2 * j + c
                if c == 0:
                    turned = pltpu.roll(noise_tile[...], turn, 1)
                for g in range(early):
                    value = capped[g, j % 2, j // 2, c]
                    value = turned[:, g * LANES : (g + 1) * LANES] - value if c == 0 else -value
                    high, low = split(value)
                    left_high[:, 2 * g * LANES : (2 * g + 1) * LANES] = high
                    left_high[:, (2 * g + 1) * LANES : (2 * g + 2) * LANES] = high
                    left_low[:, g * LANES : (g + 1) * LANES] = low
                if c == 0 and j + 1 < n_pair:
                    noise_copy(j + 1).start()
                if t >= 2:
                    early_copy(t - 2).wait()

                @pl.loop(0, pairs // cut)
                def _(step):
                    column = pl.ds(pl.multiple_of(step * cut, cut), cut)
                    both = right[:early, :, :, column].reshape(2 * early * LANES, cut)
                    high = right[:early, 0, :, column].reshape(early * LANES, cut)
                    staging[t % 2, :, column] = jnp.dot(
                        left_high[...], both, preferred_element_type=jnp.float32
                    ) + jnp.dot(left_low[...], high, preferred_element_type=jnp.float32)

                early_copy(t).start()

    for g in range(granules):
        if g == granules - 1:
            finish(early - 1)
            early_products()
        products(g)
        if g >= 1:
            cap(g - 1)
        add_partner(g)
        if g >= 1:
            hand_on(g - 1)
        if g >= 2 and g - 2 < early - 1:
            finish(g - 2)
    cap(granules - 1)
    hand_on(granules - 1)
    for g in range(early, granules):
        finish(g)
    for k in range(chunks - own):
        ring(k).wait_send()
    for g in range(early, granules):
        chol_copy(g).wait()
        capped_copy(g).wait()
    for t in range(2 * n_pair - 2, 2 * n_pair):
        early_copy(t).wait()


def bias(chol, green, noise, mean, n_field, n_pair):
    block, pairs = chol.shape
    walkers = green.shape[1]
    fields = block * n_field
    share, half = walkers // n_pair, n_pair // 2
    granules, chunks = fields // LANES, fields // math.gcd(block, LANES)
    late = 2
    early = granules - late
    dma = pltpu.SemaphoreType.DMA
    several = (granules, max(half - 1, 1))
    piece = (2, share, LANES)
    return pl.pallas_call(
        functools.partial(bias_kernel, n_field, n_pair, late),
        in_specs=[pl.BlockSpec(memory_space=pl.ANY)] * 3 + [pl.BlockSpec(memory_space=pltpu.VMEM)],
        out_specs=[pl.BlockSpec(memory_space=pltpu.VMEM)] + [pl.BlockSpec(memory_space=pl.ANY)] * 3,
        out_shape=[
            jax.ShapeDtypeStruct((2, share, fields), jnp.float32),
            jax.ShapeDtypeStruct((late, 2, LANES, pairs), jnp.bfloat16),
            jax.ShapeDtypeStruct((late, 2, half) + piece, jnp.float32),
            jax.ShapeDtypeStruct((n_pair, 2, share, pairs), jnp.float32),
        ],
        scratch_shapes=[
            pltpu.VMEM((fields, pairs), jnp.float32),
            pltpu.VMEM((2 * walkers, 2 * pairs), jnp.bfloat16),
            pltpu.VMEM((2, share, pairs), jnp.float32),
            pltpu.VMEM((granules, 2, LANES, pairs), jnp.bfloat16),
            pltpu.VMEM((granules, 2, half) + piece, jnp.float32),
            pltpu.VMEM((granules, half) + piece, jnp.float32),
            pltpu.VMEM(several + piece, jnp.float32),
            pltpu.VMEM((granules, 2, half) + piece, jnp.float32),
            pltpu.VMEM((2, fields), jnp.float32),
            pltpu.VMEM((share, fields), jnp.float32),
            pltpu.VMEM((share, 2 * early * LANES), jnp.bfloat16),
            pltpu.VMEM((share, early * LANES), jnp.bfloat16),
            dma((chunks,)), dma((chunks,)),
            dma((granules,)), dma((granules,)),
            dma(several), dma(several),
            dma((granules,)), dma((granules,)),
            dma(several), dma(several),
            dma(several), dma(several),
            dma, dma((2,)), dma((late,)), dma((late,)), dma, dma((2,)),
        ],
        compiler_params=pltpu.CompilerParams(collective_id=0, has_side_effects=True, vmem_limit_bytes=63 << 20),
    )(chol, green, noise, mean)


def operator_kernel(scale, n_field, capped_ref, noise_ref, chol_ref, early_ref, share_ref, out_ref, turned_ref, left_high, left_low):
    rows, fields = noise_ref.shape
    late, _, _, pairs = chol_ref.shape
    before = fields - late * LANES
    cut = 256 if pairs % 256 == 0 else LANES
    ahead = lax.axis_index("field") * (fields // n_field)

    @pl.when(pl.program_id(0) == 0)
    def _():
        for c in range(2):
            turned_ref[c] = pltpu.roll(share_ref[c], ahead, 1)

    noise = pltpu.roll(noise_ref[...], lax.rem(fields - ahead, fields), 1)
    for g in range(late):
        for c in range(2):
            value = capped_ref[g, 0, 0, c]
            value = noise[:, before + g * LANES : before + (g + 1) * LANES] - value if c == 0 else -value
            high, low = split(value)
            at = slice(c * rows, (c + 1) * rows)
            left_high[at, 2 * g * LANES : (2 * g + 1) * LANES] = high
            left_high[at, (2 * g + 1) * LANES : (2 * g + 2) * LANES] = high
            left_low[at, g * LANES : (g + 1) * LANES] = low

    @pl.loop(0, pairs // cut)
    def _(step):
        column = pl.ds(pl.multiple_of(step * cut, cut), cut)
        both = chol_ref[:, :, :, column].reshape(2 * late * LANES, cut)
        high = chol_ref[:, 0, :, column].reshape(late * LANES, cut)
        total = jnp.dot(left_high[...], both, preferred_element_type=jnp.float32)
        total = total + jnp.dot(left_low[...], high, preferred_element_type=jnp.float32)
        for c in range(2):
            out_ref[:, c, column] = scale * (early_ref[0, c, :, column] + total[c * rows : (c + 1) * rows])


def operator(capped, noise, chol, early, share, n_field, all_pairs):
    walkers, fields = noise.shape
    late, _, half, _, rows, _ = capped.shape
    pairs = chol.shape[3]
    scale = math.sqrt(all_pairs / fields)
    return pl.pallas_call(
        functools.partial(operator_kernel, scale, n_field),
        grid=(walkers // rows,),
        in_specs=[
            pl.BlockSpec((late, 1, 1, 2, rows, LANES), lambda i: (0, i % 2, i // 2, 0, 0, 0)),
            pl.BlockSpec((rows, fields), lambda i: (i, 0)),
            pl.BlockSpec((late, 2, LANES, pairs), lambda i: (0, 0, 0, 0)),
            pl.BlockSpec((1, 2, rows, pairs), lambda i: (i, 0, 0, 0)),
            pl.BlockSpec((2, rows, fields), lambda i: (0, 0, 0)),
        ],
        out_specs=[
            pl.BlockSpec((rows, 2, pairs), lambda i: (i, 0, 0)),
            pl.BlockSpec((2, rows, fields), lambda i: (0, 0, 0)),
        ],
        out_shape=[
            jax.ShapeDtypeStruct((walkers, 2, pairs), jnp.float32),
            jax.ShapeDtypeStruct((2, rows, fields), jnp.float32),
        ],
        scratch_shapes=[
            pltpu.VMEM((2 * rows, 2 * late * LANES), jnp.bfloat16),
            pltpu.VMEM((2 * rows, late * LANES), jnp.bfloat16),
        ],
        compiler_params=pltpu.CompilerParams(vmem_limit_bytes=60 << 20),
    )(capped, noise, chol, early, share)


def per_device(n_field, n_pair, cholesky_tensor, green_function, mean_field, field_noise):
    share, chol, capped, early = bias(cholesky_tensor, green_function, field_noise, mean_field, n_field, n_pair)
    all_pairs = cholesky_tensor.shape[1] * n_pair
    one_body, turned = operator(capped, field_noise, chol, early, share, n_field, all_pairs)
    return turned, one_body


def solution(mesh):
    return jax.shard_map(
        functools.partial(per_device, mesh.shape["field"], mesh.shape["pair"]),
        mesh=mesh,
        in_specs=(
            P(("grp", "field"), "pair"),
            P(None, ("grp", "field"), "pair"),
            P(None, "grp"),
            P(("grp", "field"), None),
        ),
        out_specs=(P(None, ("grp", "field", "pair"), None), P(("grp", "field"), None, "pair")),
        check_vma=False,
    )
```

profile of v0, /device:TPU:0, one launch (start us, length us, event | category | flops | bytes accessed | tf_op | source)
XLA Modules:
  0.0 196.1 jit_solution(15165904157995114778)
XLA Ops:
  0.6 170.2 %shard_map.59 = (f32[2,256,768]{2,1,0:T(8,128)}, bf16[2,2,128,2304]{3,2,1,0:T(8,128)(2,1)}, f32[2,2,2,2,256,128]{5,4,3,2,1,0:T(8,128)}, f32[4,2,256,2304]{3,2,1,0:T(8,128)}) custom-call(f32[192,2304]{1,0:T(8,128)} %chol_in.1, f32[2,1024,2304]{2,1,0:T(8,128)} %green.1, f32[1024,768]{1,0:T(8,128)} %noise_ref.1, f32[2,768]{1,0:T(2,128)} %mean_ref.1), custom_call_target="tpu_custom_call" | custom-call | tf_op jit(solution)/shard_map/pallas_call | solution.py:250
  170.8 25.3 %shard_map.60 = (f32[1024,2,2304]{2,1,0:T(2,128)}, f32[2,256,768]{2,1,0:T(8,128)}) custom-call(f32[2,2,2,2,256,128]{5,4,3,2,1,0:T(8,128)} %get-tuple-element.8.capped_ref, f32[1024,768]{1,0:T(8,128)} %noise_ref.1, bf16[2,2,128,2304]{3,2,1,0:T(8,128)(2,1)} %get-tuple-element.9.chol_ref, f32[4,2,256,2304]{3,2,1,0:T(8,128)} %get-tuple-element.10.early_ref, ...), custom_call_target="tpu_custom_call" | custom-call | tf_op jit(solution)/shard_map/pallas_call | solution.py:324
where the time goes:
time: 196 us
  Pallas kernels  195 us (99%)
    pallas_call x1, Pallas kernels, bias(): pl.pallas_call(functools.partial(bias_kernel, n_field, n_pair, late), in_...  170 us
    pallas_call x1, Pallas kernels, operator(): pl.pallas_call(functools.partial(operator_kernel, scale, n_field), grid=(...  25.3 us

commit v1 on v0

--- a/solution.py
+++ b/solution.py
@@ -19,14 +19,20 @@
 MESH = pl.DeviceIdType.MESH
 
 
+def stacked(right, granules, column):
+    wide = right[:granules, :, :, column]
+    high = right[:granules, 0, :, column]
+    return jnp.concatenate([wide.reshape(-1, wide.shape[3]), high.reshape(-1, high.shape[2])], axis=0)
+
+
 def bias_kernel(
     n_field, n_pair, late, chol_in, green, noise, mean_ref, share_ref, chol_out, capped_out, early_out,
-    stack, green_split, staging, right, part, first, second, capped, mean_turned, noise_tile, left_high, left_low,
+    stack, green_split, staging, right, part, first, second, capped, mean_turned, noise_tile, left,
     ring_send, ring_recv, part_send, part_recv, sum_send, sum_recv, own_send, own_recv,
     peer_send, peer_recv, pass_send, pass_recv, load_sem, green_sem, chol_sem, capped_sem, noise_sem, early_sem,
 ):
     fields, pairs = stack.shape
-    share = share_ref.shape[1]
+    share, slots = share_ref.shape[1], staging.shape[0]
     block = chol_in.shape[0]
     chunk = math.gcd(block, LANES)
     chunks, own = fields // chunk, block // chunk
@@ -75,18 +81,19 @@
 
     def fetch(t):
         j, c = t // 2, t % 2
-        return pltpu.make_async_copy(green.at[c, pl.ds(j * share, share)], staging.at[t % 2], green_sem.at[t % 2])
-
-    fetch(0).start()
+        return pltpu.make_async_copy(green.at[c, pl.ds(j * share, share)], staging.at[t % slots], green_sem.at[t % slots])
+
+    for t in range(slots - 1):
+        fetch(t).start()
     for t in range(2 * n_pair):
-        if t + 1 < 2 * n_pair:
-            fetch(t + 1).start()
+        if t + slots - 1 < 2 * n_pair:
+            fetch(t + slots - 1).start()
         fetch(t).wait()
 
         @pl.loop(0, share // 16)
         def _(step):
             at = pl.multiple_of(step * 16, 16)
-            high, low = split(staging[t % 2, pl.ds(at, 16), :])
+            high, low = split(staging[t % slots, pl.ds(at, 16), :])
             into = pl.multiple_of(t * share + at, 16)
             green_split[pl.ds(into, 16), :pairs] = high
             green_split[pl.ds(into, 16), pairs:] = low
@@ -132,17 +139,24 @@
         if g >= early:
             chol_copy(g).start()
 
-        @pl.loop(0, n_pair)
-        def _(j):
-            rows = pl.ds(pl.multiple_of(j * 2 * share, 16), 2 * share)
+        def product(side, at):
+            rows = pl.ds(pl.multiple_of((2 * at + side) * 2 * share, 16), 2 * share)
             dims = (((1,), (1,)), ((), ()))
             pair_of = right[g].reshape(2 * LANES, pairs)
             both = lax.dot_general(green_split[rows, :pairs], pair_of, dims, preferred_element_type=jnp.float32)
             cross = lax.dot_general(green_split[rows, pairs:], right[g, 0], dims, preferred_element_type=jnp.float32)
             total = both[:, :LANES] + both[:, LANES:] + cross
-            part[g, lax.rem(j, 2), j // 2] = total.reshape(2, share, LANES)
+            part[g, side, at] = total.reshape(2, share, LANES)
+
+        @pl.loop(0, half)
+        def _(at):
+            product(1 - core, at)
 
         part_copy(g).start()
+
+        @pl.loop(0, half)
+        def _(step):
+            product(core, lax.rem(hop + 1 + step, half))
 
     def add_partner(g):
         part_copy(g).wait()
@@ -178,61 +192,64 @@
             capped_copy(g).start()
 
     def early_copy(t):
-        return pltpu.make_async_copy(staging.at[t % 2], early_out.at[t // 2, t % 2], early_sem.at[t % 2])
-
-    def early_products():
+        return pltpu.make_async_copy(staging.at[t % slots], early_out.at[t // 2, t % 2], early_sem.at[t % slots])
+
+    def early_product(j):
         cut = 256 if pairs % 256 == 0 else LANES
-        for j in range(n_pair):
-            noise_copy(j).wait()
+        noise_copy(j).wait()
+        for c in range(2):
+            at = slice(c * share, (c + 1) * share)
+            if c == 0:
+                turned = pltpu.roll(noise_tile[...], turn, 1)
+            for g in range(early):
+                value = capped[g, j % 2, j // 2, c]
+                value = turned[:, g * LANES : (g + 1) * LANES] - value if c == 0 else -value
+                high, low = split(value)
+                left[at, 2 * g * LANES : (2 * g + 1) * LANES] = high
+                left[at, (2 * g + 1) * LANES : (2 * g + 2) * LANES] = high
+                left[at, (2 * early + g) * LANES : (2 * early + g + 1) * LANES] = low
+        if j + 1 < n_pair:
+            noise_copy(j + 1).start()
+        for t in range(2 * j, 2 * j + 2):
+            if t >= slots:
+                early_copy(t - slots).wait()
+
+        @pl.loop(0, pairs // cut)
+        def _(step):
+            column = pl.ds(pl.multiple_of(step * cut, cut), cut)
+            total = jnp.dot(left[...], stacked(right, early, column), preferred_element_type=jnp.float32)
             for c in range(2):
-                t = 2 * j + c
-                if c == 0:
-                    turned = pltpu.roll(noise_tile[...], turn, 1)
-                for g in range(early):
-                    value = capped[g, j % 2, j // 2, c]
-                    value = turned[:, g * LANES : (g + 1) * LANES] - value if c == 0 else -value
-                    high, low = split(value)
-                    left_high[:, 2 * g * LANES : (2 * g + 1) * LANES] = high
-                    left_high[:, (2 * g + 1) * LANES : (2 * g + 2) * LANES] = high
-                    left_low[:, g * LANES : (g + 1) * LANES] = low
-                if c == 0 and j + 1 < n_pair:
-                    noise_copy(j + 1).start()
-                if t >= 2:
-                    early_copy(t - 2).wait()
-
-                @pl.loop(0, pairs // cut)
-                def _(step):
-                    column = pl.ds(pl.multiple_of(step * cut, cut), cut)
-                    both = right[:early, :, :, column].reshape(2 * early * LANES, cut)
-                    high = right[:early, 0, :, column].reshape(early * LANES, cut)
-                    staging[t % 2, :, column] = jnp.dot(
-                        left_high[...], both, preferred_element_type=jnp.float32
-                    ) + jnp.dot(left_low[...], high, preferred_element_type=jnp.float32)
-
-                early_copy(t).start()
+                staging[(2 * j + c) % slots, :, column] = total[c * share : (c + 1) * share]
+
+        for t in range(2 * j, 2 * j + 2):
+            early_copy(t).start()
+
+    def exchange(g, between):
+        add_partner(g)
+        between(0)
+        cap(g)
+        between(1)
+        hand_on(g)
+        between(2)
+        finish(g)
+
+    per_step = pl.cdiv(n_pair, 4)
+
+    def some(step):
+        for j in range(step * per_step, min((step + 1) * per_step, n_pair)):
+            early_product(j)
 
     for g in range(granules):
-        if g == granules - 1:
-            finish(early - 1)
-            early_products()
         products(g)
-        if g >= 1:
-            cap(g - 1)
-        add_partner(g)
-        if g >= 1:
-            hand_on(g - 1)
-        if g >= 2 and g - 2 < early - 1:
-            finish(g - 2)
-    cap(granules - 1)
-    hand_on(granules - 1)
-    for g in range(early, granules):
-        finish(g)
+        exchange(g, some if g == early else lambda step: None)
+        if g == early:
+            some(3)
     for k in range(chunks - own):
         ring(k).wait_send()
     for g in range(early, granules):
         chol_copy(g).wait()
         capped_copy(g).wait()
-    for t in range(2 * n_pair - 2, 2 * n_pair):
+    for t in range(max(2 * n_pair - slots, 0), 2 * n_pair):
         early_copy(t).wait()
 
 
@@ -260,7 +277,7 @@
         scratch_shapes=[
             pltpu.VMEM((fields, pairs), jnp.float32),
             pltpu.VMEM((2 * walkers, 2 * pairs), jnp.bfloat16),
-            pltpu.VMEM((2, share, pairs), jnp.float32),
+            pltpu.VMEM((4, share, pairs), jnp.float32),
             pltpu.VMEM((granules, 2, LANES, pairs), jnp.bfloat16),
             pltpu.VMEM((granules, 2, half) + piece, jnp.float32),
             pltpu.VMEM((granules, half) + piece, jnp.float32),
@@ -268,21 +285,20 @@
             pltpu.VMEM((granules, 2, half) + piece, jnp.float32),
             pltpu.VMEM((2, fields), jnp.float32),
             pltpu.VMEM((share, fields), jnp.float32),
-            pltpu.VMEM((share, 2 * early * LANES), jnp.bfloat16),
-            pltpu.VMEM((share, early * LANES), jnp.bfloat16),
+            pltpu.VMEM((2 * share, 3 * early * LANES), jnp.bfloat16),
             dma((chunks,)), dma((chunks,)),
             dma((granules,)), dma((granules,)),
             dma(several), dma(several),
             dma((granules,)), dma((granules,)),
             dma(several), dma(several),
             dma(several), dma(several),
-            dma, dma((2,)), dma((late,)), dma((late,)), dma, dma((2,)),
+            dma, dma((4,)), dma((late,)), dma((late,)), dma, dma((4,)),
         ],
         compiler_params=pltpu.CompilerParams(collective_id=0, has_side_effects=True, vmem_limit_bytes=63 << 20),
     )(chol, green, noise, mean)
 
 
-def operator_kernel(scale, n_field, capped_ref, noise_ref, chol_ref, early_ref, share_ref, out_ref, turned_ref, left_high, left_low):
+def operator_kernel(scale, n_field, capped_ref, noise_ref, chol_ref, early_ref, share_ref, out_ref, turned_ref, left):
     rows, fields = noise_ref.shape
     late, _, _, pairs = chol_ref.shape
     before = fields - late * LANES
@@ -301,17 +317,13 @@
             value = noise[:, before + g * LANES : before + (g + 1) * LANES] - value if c == 0 else -value
             high, low = split(value)
             at = slice(c * rows, (c + 1) * rows)
-            left_high[at, 2 * g * LANES : (2 * g + 1) * LANES] = high
-            left_high[at, (2 * g + 1) * LANES : (2 * g + 2) * LANES] = high
-            left_low[at, g * LANES : (g + 1) * LANES] = low
-
-    @pl.loop(0, pairs // cut)
-    def _(step):
-        column = pl.ds(pl.multiple_of(step * cut, cut), cut)
-        both = chol_ref[:, :, :, column].reshape(2 * late * LANES, cut)
-        high = chol_ref[:, 0, :, column].reshape(late * LANES, cut)
-        total = jnp.dot(left_high[...], both, preferred_element_type=jnp.float32)
-        total = total + jnp.dot(left_low[...], high, preferred_element_type=jnp.float32)
+            left[at, 2 * g * LANES : (2 * g + 1) * LANES] = high
+            left[at, (2 * g + 1) * LANES : (2 * g + 2) * LANES] = high
+            left[at, (2 * late + g) * LANES : (2 * late + g + 1) * LANES] = low
+
+    for step in range(pairs // cut):
+        column = slice(step * cut, (step + 1) * cut)
+        total = jnp.dot(left[...], stacked(chol_ref, late, column), preferred_element_type=jnp.float32)
         for c in range(2):
             out_ref[:, c, column] = scale * (early_ref[0, c, :, column] + total[c * rows : (c + 1) * rows])
 
@@ -340,8 +352,7 @@
             jax.ShapeDtypeStruct((2, rows, fields), jnp.float32),
         ],
         scratch_shapes=[
-            pltpu.VMEM((2 * rows, 2 * late * LANES), jnp.bfloat16),
-            pltpu.VMEM((2 * rows, late * LANES), jnp.bfloat16),
+            pltpu.VMEM((2 * rows, 3 * late * LANES), jnp.bfloat16),
         ],
         compiler_params=pltpu.CompilerParams(vmem_limit_bytes=60 << 20),
     )(capped, noise, chol, early, share)

time: 196 us -> 179 us (0.913)
  Pallas kernels: 195 us -> 178 us
    pallas_call x1, Pallas kernels: 170 us -> 156 us  [bias(): pl.pallas_call(functools.partial(bias_kernel, n_field, n_pair, late), in_...]
    pallas_call x1, Pallas kernels: 25.3 us -> 21.5 us  [operator(): pl.pallas_call(functools.partial(operator_kernel, scale, n_field), grid=(...]
where the time goes in v1:
time: 179 us; the launch traced here: 178 us
  Pallas kernels  178 us (99%)
    pallas_call x1, Pallas kernels, bias(): pl.pallas_call(functools.partial(bias_kernel, n_field, n_pair, late), in_...  156 us
    pallas_call x1, Pallas kernels, operator(): pl.pallas_call(functools.partial(operator_kernel, scale, n_field), grid=(...  21.5 us

profile of v1, /device:TPU:0, one launch (start us, length us, event | category | flops | bytes accessed | tf_op | source)
XLA Modules:
  0.0 178.3 jit_solution(18149149359085719808)
XLA Ops:
  0.6 156.1 %shard_map.59 = (f32[2,256,768]{2,1,0:T(8,128)}, bf16[2,2,128,2304]{3,2,1,0:T(8,128)(2,1)}, f32[2,2,2,2,256,128]{5,4,3,2,1,0:T(8,128)}, f32[4,2,256,2304]{3,2,1,0:T(8,128)}) custom-call(f32[192,2304]{1,0:T(8,128)} %chol_in.1, f32[2,1024,2304]{2,1,0:T(8,128)} %green.1, f32[1024,768]{1,0:T(8,128)} %noise_ref.1, f32[2,768]{1,0:T(2,128)} %mean_ref.1), custom_call_target="tpu_custom_call" | custom-call | tf_op jit(solution)/shard_map/pallas_call | solution.py:267
  156.8 21.5 %shard_map.60 = (f32[1024,2,2304]{2,1,0:T(2,128)}, f32[2,256,768]{2,1,0:T(8,128)}) custom-call(f32[2,2,2,2,256,128]{5,4,3,2,1,0:T(8,128)} %get-tuple-element.8.capped_ref, f32[1024,768]{1,0:T(8,128)} %noise_ref.1, bf16[2,2,128,2304]{3,2,1,0:T(8,128)(2,1)} %get-tuple-element.9.chol_ref, f32[4,2,256,2304]{3,2,1,0:T(8,128)} %get-tuple-element.10.early_ref, ...), custom_call_target="tpu_custom_call" | custom-call | tf_op jit(solution)/shard_map/pallas_call | solution.py:336

commit v2 on v1

--- a/solution.py
+++ b/solution.py
@@ -100,24 +100,24 @@
 
     load.wait()
 
-    def part_copy(g):
-        return remote(part.at[g, 1 - core], first.at[g], part_send.at[g], part_recv.at[g], partner_id)
-
-    def sum_copy(g, d):
-        source = part.at[g, core, peer_hop(d)]
-        return remote(source, second.at[g, d - 1], sum_send.at[g, d - 1], sum_recv.at[g, d - 1], peer_id(d))
+    def part_copy(g, at):
+        return remote(part.at[g, 1 - core, at], first.at[g, at], part_send.at[g, at], part_recv.at[g, at], partner_id)
+
+    def sum_copy(g, d, c):
+        source, at = part.at[g, core, peer_hop(d), c], (g, d - 1, c)
+        return remote(source, second.at[at], sum_send.at[at], sum_recv.at[at], peer_id(d))
 
     def own_copy(g):
         at = capped.at[g, core, hop]
         return remote(at, at, own_send.at[g], own_recv.at[g], partner_id)
 
-    def peer_copy(g, d):
-        at = capped.at[g, core, hop]
-        return remote(at, at, peer_send.at[g, d - 1], peer_recv.at[g, d - 1], peer_id(d))
-
-    def pass_copy(g, d):
-        at = capped.at[g, core, peer_hop(half - d)]
-        return remote(at, at, pass_send.at[g, d - 1], pass_recv.at[g, d - 1], partner_id)
+    def peer_copy(g, d, c):
+        at, sem = capped.at[g, core, hop, c], (g, d - 1, c)
+        return remote(at, at, peer_send.at[sem], peer_recv.at[sem], peer_id(d))
+
+    def pass_copy(g, d, c):
+        at, sem = capped.at[g, core, peer_hop(half - d), c], (g, d - 1, c)
+        return remote(at, at, pass_send.at[sem], pass_recv.at[sem], partner_id)
 
     def chol_copy(g):
         return pltpu.make_async_copy(right.at[g], chol_out.at[g - early], chol_sem.at[g - early])
@@ -125,12 +125,18 @@
     def capped_copy(g):
         return pltpu.make_async_copy(capped.at[g], capped_out.at[g - early], capped_sem.at[g - early])
 
+    def pump(end):
+        while passed[0] < min(end, chunks):
+            k = passed[0]
+            ring(k - own).wait_recv()
+            if k + own < chunks:
+                ring(k).start()
+            passed[0] += 1
+
+    passed = [own]
+
     def products(g):
-        for k in range(g * per_granule, (g + 1) * per_granule):
-            if k >= own:
-                ring(k - own).wait_recv()
-                if k + own < chunks:
-                    ring(k).start()
+        pump((g + 1) * per_granule)
         step_rows = 32
         for at in range(0, LANES, step_rows):
             high, low = split(stack[g * LANES + at : g * LANES + at + step_rows, :])
@@ -149,45 +155,48 @@
             part[g, side, at] = total.reshape(2, share, LANES)
 
         @pl.loop(0, half)
-        def _(at):
+        def _(step):
+            at = peer_hop(step + 1)
             product(1 - core, at)
-
-        part_copy(g).start()
+            part_copy(g, at).start()
 
         @pl.loop(0, half)
         def _(step):
-            product(core, lax.rem(hop + 1 + step, half))
-
-    def add_partner(g):
-        part_copy(g).wait()
-        for d in list(range(1, half)) + [0]:
-            at = peer_hop(d)
+            at = peer_hop(step + 1)
+            product(core, at)
+            part_copy(g, at).wait()
             part[g, core, at] = part[g, core, at] + first[g, at]
-            if d:
-                sum_copy(g, d).start()
+
+            @pl.when(step < half - 1)
+            def _():
+                for c in range(2):
+                    sum_copy(g, step + 1, c).start()
 
     def cap(g):
-        total = part[g, core, hop]
-        for d in range(1, half):
-            sum_copy(g, d).wait()
-            total = total + second[g, d - 1]
         columns = slice(g * LANES, (g + 1) * LANES)
-        value = 2.0 * jnp.tanh((total - mean_turned[:, columns][:, None, :]) / 2.0)
-        capped[g, core, hop] = value
-        share_ref[:, :, columns] = value
-        for d in range(1, half):
-            peer_copy(g, d).start()
+        for c in range(2):
+            total = part[g, core, hop, c]
+            for d in range(1, half):
+                sum_copy(g, d, c).wait()
+                total = total + second[g, d - 1, c]
+            value = 2.0 * jnp.tanh((total - mean_turned[c : c + 1, columns]) / 2.0)
+            capped[g, core, hop, c] = value
+            share_ref[c, :, columns] = value
+            for d in range(1, half):
+                peer_copy(g, d, c).start()
         own_copy(g).start()
 
     def hand_on(g):
-        for d in range(1, half):
-            peer_copy(g, d).wait()
-            pass_copy(g, d).start()
+        for c in range(2):
+            for d in range(1, half):
+                peer_copy(g, d, c).wait()
+                pass_copy(g, d, c).start()
 
     def finish(g):
         own_copy(g).wait()
-        for d in range(1, half):
-            pass_copy(g, d).wait()
+        for c in range(2):
+            for d in range(1, half):
+                pass_copy(g, d, c).wait()
         if g >= early:
             capped_copy(g).start()
 
@@ -224,26 +233,36 @@
         for t in range(2 * j, 2 * j + 2):
             early_copy(t).start()
 
-    def exchange(g, between):
-        add_partner(g)
-        between(0)
-        cap(g)
-        between(1)
-        hand_on(g)
-        between(2)
-        finish(g)
-
     per_step = pl.cdiv(n_pair, 4)
 
     def some(step):
         for j in range(step * per_step, min((step + 1) * per_step, n_pair)):
             early_product(j)
 
-    for g in range(granules):
+    products(0)
+    for g in range(1, granules):
         products(g)
-        exchange(g, some if g == early else lambda step: None)
+        if g == 1:
+            cap(0)
+            cap(1)
+            pump(2 * per_granule + per_granule // 2)
+            hand_on(0)
+            hand_on(1)
+            finish(0)
+            continue
+        finish(g - 1)
         if g == early:
+            some(0)
+        cap(g)
+        if g == early:
+            some(1)
+        elif g < early:
+            pump((g + 1) * per_granule + per_granule // 2)
+        hand_on(g)
+        if g == early:
+            some(2)
             some(3)
+    finish(granules - 1)
     for k in range(chunks - own):
         ring(k).wait_send()
     for g in range(early, granules):
@@ -262,7 +281,7 @@
     late = 2
     early = granules - late
     dma = pltpu.SemaphoreType.DMA
-    several = (granules, max(half - 1, 1))
+    several = (granules, max(half - 1, 1), 2)
     piece = (2, share, LANES)
     return pl.pallas_call(
         functools.partial(bias_kernel, n_field, n_pair, late),
@@ -281,13 +300,13 @@
             pltpu.VMEM((granules, 2, LANES, pairs), jnp.bfloat16),
             pltpu.VMEM((granules, 2, half) + piece, jnp.float32),
             pltpu.VMEM((granules, half) + piece, jnp.float32),
-            pltpu.VMEM(several + piece, jnp.float32),
+            pltpu.VMEM(several[:2] + piece, jnp.float32),
             pltpu.VMEM((granules, 2, half) + piece, jnp.float32),
             pltpu.VMEM((2, fields), jnp.float32),
             pltpu.VMEM((share, fields), jnp.float32),
             pltpu.VMEM((2 * share, 3 * early * LANES), jnp.bfloat16),
             dma((chunks,)), dma((chunks,)),
-            dma((granules,)), dma((granules,)),
+            dma((granules, half)), dma((granules, half)),
             dma(several), dma(several),
             dma((granules,)), dma((granules,)),
             dma(several), dma(several),

time: 179 us -> 169 us (0.944)
  Pallas kernels: 178 us -> 168 us
    pallas_call x1, Pallas kernels: 156 us -> 146 us  [bias(): pl.pallas_call(functools.partial(bias_kernel, n_field, n_pair, late), in_...]
where the time goes in v2:
time: 169 us
  Pallas kernels  168 us (99%)
    pallas_call x1, Pallas kernels, bias(): pl.pallas_call(functools.partial(bias_kernel, n_field, n_pair, late), in_...  146 us
    pallas_call x1, Pallas kernels, operator(): pl.pallas_call(functools.partial(operator_kernel, scale, n_field), grid=(...  21.5 us

profile of v2, /device:TPU:0, one launch (start us, length us, event | category | flops | bytes accessed | tf_op | source)
XLA Modules:
  0.0 168.6 jit_solution(8742498037118841626)
XLA Ops:
  0.6 146.5 %shard_map.59 = (f32[2,256,768]{2,1,0:T(8,128)}, bf16[2,2,128,2304]{3,2,1,0:T(8,128)(2,1)}, f32[2,2,2,2,256,128]{5,4,3,2,1,0:T(8,128)}, f32[4,2,256,2304]{3,2,1,0:T(8,128)}) custom-call(f32[192,2304]{1,0:T(8,128)} %chol_in.1, f32[2,1024,2304]{2,1,0:T(8,128)} %green.1, f32[1024,768]{1,0:T(8,128)} %noise_ref.1, f32[2,768]{1,0:T(2,128)} %mean_ref.1), custom_call_target="tpu_custom_call" | custom-call | tf_op jit(solution)/shard_map/pallas_call | solution.py:286
  147.1 21.5 %shard_map.60 = (f32[1024,2,2304]{2,1,0:T(2,128)}, f32[2,256,768]{2,1,0:T(8,128)}) custom-call(f32[2,2,2,2,256,128]{5,4,3,2,1,0:T(8,128)} %get-tuple-element.8.capped_ref, f32[1024,768]{1,0:T(8,128)} %noise_ref.1, bf16[2,2,128,2304]{3,2,1,0:T(8,128)(2,1)} %get-tuple-element.9.chol_ref, f32[4,2,256,2304]{3,2,1,0:T(8,128)} %get-tuple-element.10.early_ref, ...), custom_call_target="tpu_custom_call" | custom-call | tf_op jit(solution)/shard_map/pallas_call | solution.py:355

commit v3 on v2

--- a/solution.py
+++ b/solution.py
@@ -250,18 +250,17 @@
             hand_on(1)
             finish(0)
             continue
+        if g > early:
+            some(2 * (g - early))
         finish(g - 1)
         if g == early:
             some(0)
         cap(g)
-        if g == early:
-            some(1)
-        elif g < early:
+        if g >= early:
+            some(2 * (g - early) + 1)
+        else:
             pump((g + 1) * per_granule + per_granule // 2)
         hand_on(g)
-        if g == early:
-            some(2)
-            some(3)
     finish(granules - 1)
     for k in range(chunks - own):
         ring(k).wait_send()

time: 169 us -> 165 us (0.976)
  Pallas kernels: 168 us -> 164 us
    pallas_call x1, Pallas kernels: 146 us -> 143 us  [bias(): pl.pallas_call(functools.partial(bias_kernel, n_field, n_pair, late), in_...]
where the time goes in v3:
time: 165 us
  Pallas kernels  164 us (99%)
    pallas_call x1, Pallas kernels, bias(): pl.pallas_call(functools.partial(bias_kernel, n_field, n_pair, late), in_...  143 us
    pallas_call x1, Pallas kernels, operator(): pl.pallas_call(functools.partial(operator_kernel, scale, n_field), grid=(...  21.5 us

profile of v3, /device:TPU:0, one launch (start us, length us, event | category | flops | bytes accessed | tf_op | source)
XLA Modules:
  0.0 164.9 jit_solution(5770748735133458196)
XLA Ops:
  0.6 142.7 %shard_map.59 = (f32[2,256,768]{2,1,0:T(8,128)}, bf16[2,2,128,2304]{3,2,1,0:T(8,128)(2,1)}, f32[2,2,2,2,256,128]{5,4,3,2,1,0:T(8,128)}, f32[4,2,256,2304]{3,2,1,0:T(8,128)}) custom-call(f32[192,2304]{1,0:T(8,128)} %chol_in.1, f32[2,1024,2304]{2,1,0:T(8,128)} %green.1, f32[1024,768]{1,0:T(8,128)} %noise_ref.1, f32[2,768]{1,0:T(2,128)} %mean_ref.1), custom_call_target="tpu_custom_call" | custom-call | tf_op jit(solution)/shard_map/pallas_call | solution.py:285
  143.4 21.5 %shard_map.60 = (f32[1024,2,2304]{2,1,0:T(2,128)}, f32[2,256,768]{2,1,0:T(8,128)}) custom-call(f32[2,2,2,2,256,128]{5,4,3,2,1,0:T(8,128)} %get-tuple-element.8.capped_ref, f32[1024,768]{1,0:T(8,128)} %noise_ref.1, bf16[2,2,128,2304]{3,2,1,0:T(8,128)(2,1)} %get-tuple-element.9.chol_ref, f32[4,2,256,2304]{3,2,1,0:T(8,128)} %get-tuple-element.10.early_ref, ...), custom_call_target="tpu_custom_call" | custom-call | tf_op jit(solution)/shard_map/pallas_call | solution.py:354
